TPU v7x, 128 devices: a whole 4x4x4 slice. The times are simulated.
128 devices in a mesh: grp: 8 (over z_lo, x), obs: 16 (over y, z_hi, core).
Axes of the slice: x: 4, y: 4, z: 4 (z_hi: 2, z_lo: 2; z = z_hi * 2 + z_lo), core: 2. Of those that a mesh axis runs over, the one named last changes fastest.
Arguments:
- signals: bfloat16 [4, 256, 131072], P(None, None, ('grp', 'obs')), may hold values from -6 to 6
- patch_count: int32 [128], P(('grp', 'obs')), may hold values from 0 to 8, as said below
- patch_place: int32 [1024], P(('grp', 'obs')), may hold values from 0 to 63, as said below
- face_geom: float32 [4, 65536], P(None, ('grp', 'obs')), may hold values from -3.5 to 30, as said below
- obs_pos: float32 [3, 4096], P(None, 'obs'), may hold values from -60 to 60, as said below
Outputs:
- pressure: float32 [16, 4096], P('grp', 'obs')
Inputs may be any that keep to these rules, and one draw needn't show every extreme that they name: `patch_count`: each partition holds 0 to 8 live patches; in every face group the counts sum to 64 and some partition holds exactly 8. `patch_place`: A live slot names owner o and patch j of the partition's group as o * 4 + j; within a group every such value is named by exactly one live slot, so every owner receives exactly 4 patches; no partition holds two live patches of the same owner. Slots beyond the count hold arbitrary values in the range. `face_geom`: faces lie on a surface around the first coordinate's axis: the first coordinate between 0 and 30, the distance from that axis between 2 and 3.5; the area lies between 0.5 and 10. `obs_pos`: every observer lies 25 to 60 from the anchor (0, 0, 0) and 8 or more from the first coordinate's axis.
All inputs are finite; a program needn't handle non-finite values.
Results may differ from a plain program's by a relative error of at most 0.004.
Values may be sent and summed in bfloat16 or wider, within the bound.
No kernel may reach another device: no remote copies, remote signals or barrier semaphores. Data moves between devices by JAX's collectives and lax.ppermute only.
A program may use at most 64 MiB of HBM per device.

v0:
```python
import math
import jax
import jax.numpy as jnp
from jax import lax
from jax.sharding import PartitionSpec as P

SAMPLES = 256
NFREQ = 8
NSIG = 4
PATCH = 128
MAXP = 8
PER_OWN = 4
FACES_OWN = 512
omega_step = 0.5
four_pi = 4.0 * math.pi


def spectral_basis(samples, freq_count):
    sample_idx = jnp.arange(samples, dtype=jnp.float32)
    harmonic = jnp.arange(1, freq_count + 1, dtype=jnp.float32)
    angles = 2.0 * math.pi / samples * (sample_idx[:, None] * harmonic[None, :])
    window = (0.5 - 0.5 * jnp.cos(2.0 * math.pi / samples * sample_idx)) * math.sqrt(
        8.0 / (3.0 * samples)
    )
    table = jnp.concatenate(
        [window[:, None] * jnp.cos(angles), -window[:, None] * jnp.sin(angles)], axis=1
    )
    return table.astype(jnp.bfloat16)


def pressure_tiles(observers, spectra, geometry):
    freq_count = spectra.shape[0] // 8
    wavenumber = omega_step * jnp.arange(1, freq_count + 1, dtype=jnp.float32)
    values = spectra.reshape(4, 2, freq_count, spectra.shape[1])
    separation = observers[:, :, None] - geometry[:3, None, :]
    dist_sq = jnp.sum(separation * separation, axis=0)
    distance = jnp.sqrt(dist_sq)
    inv_sq = 1.0 / dist_sq
    load_re = jnp.zeros((freq_count,) + dist_sq.shape, jnp.float32)
    load_im = jnp.zeros((freq_count,) + dist_sq.shape, jnp.float32)
    for coord in range(3):
        load_re = load_re + values[1 + coord, 0][:, None, :] * separation[coord][None]
        load_im = load_im + values[1 + coord, 1][:, None, :] * separation[coord][None]
    dip_re = load_re * inv_sq[None]
    dip_im = load_im * inv_sq[None]
    omega_grid = wavenumber[:, None, None]
    phase = omega_grid * distance[None]
    mono_re = values[0, 0][:, None, :]
    mono_im = values[0, 1][:, None, :]
    bracket_re = -omega_grid * mono_im + dip_re - phase * dip_im
    bracket_im = omega_grid * mono_re + dip_im + phase * dip_re
    amplitude = (geometry[3][None, :] / (four_pi * distance))[None]
    green_re = amplitude * jnp.cos(phase)
    green_im = -amplitude * jnp.sin(phase)
    press_re = jnp.sum(green_re * bracket_re - green_im * bracket_im, axis=2)
    press_im = jnp.sum(green_re * bracket_im + green_im * bracket_re, axis=2)
    return jnp.concatenate([press_re, press_im], axis=0)


def accumulate(observers, spectra, geometry):
    face_count = spectra.shape[1]
    block_len = face_count
    while block_len > 128 and (
        block_len * observers.shape[1] > 131072 or face_count % block_len != 0
    ):
        block_len = block_len // 2
    step_count = face_count // block_len
    spec_blocks = spectra.reshape(spectra.shape[0], step_count, block_len).transpose(1, 0, 2)
    geom_blocks = geometry.reshape(4, step_count, block_len).transpose(1, 0, 2)

    def add_block(running, pieces):
        return (running + pressure_tiles(observers, pieces[0], pieces[1]), None)

    zero_sum = jnp.zeros((spectra.shape[0] // 4, observers.shape[1]), jnp.float32)
    result, _ = lax.scan(add_block, zero_sum, (spec_blocks, geom_blocks))
    return result


def local(signals, patch_count, patch_place, face_geom, obs_pos):
    owners = lax.axis_size("obs")
    channels = NSIG * 2 * NFREQ
    dft_basis = spectral_basis(SAMPLES, NFREQ).astype(jnp.float32)
    slot_index = jnp.arange(MAXP, dtype=jnp.int32)
    is_live = slot_index < patch_count[0]
    target_owner = patch_place // PER_OWN
    target_part = patch_place % PER_OWN
    owner_index = jnp.arange(owners, dtype=jnp.int32)
    picked = jnp.logical_and(target_owner[None, :] == owner_index[:, None], is_live[None, :])
    header = jnp.where(
        jnp.any(picked, axis=1), jnp.sum(jnp.where(picked, target_part[None, :], 0), axis=1), -1
    )
    select = picked.astype(jnp.bfloat16)
    row_blocks = signals.reshape(NSIG, SAMPLES, MAXP, PATCH)
    outgoing = jnp.einsum(
        "om,stmp->ostp", select, row_blocks, preferred_element_type=jnp.float32
    ).astype(jnp.bfloat16)
    arrived_rows, senders = (
        lax.all_to_all(outgoing, "obs", split_axis=0, concat_axis=0, tiled=True),
        lax.all_to_all(header, "obs", split_axis=0, concat_axis=0, tiled=True),
    )
    arrived = jnp.einsum(
        "ostp,tc->oscp",
        arrived_rows.astype(jnp.float32),
        dft_basis,
        precision=lax.Precision.HIGHEST,
    ).astype(jnp.bfloat16)
    arrived = arrived.reshape(owners, channels, PATCH)
    owned_part = (senders[:, None] == jnp.arange(PER_OWN, dtype=jnp.int32)[None, :]).astype(
        jnp.bfloat16
    )
    face_spec = jnp.einsum(
        "oj,okp->kjp", owned_part, arrived, preferred_element_type=jnp.float32
    ).astype(jnp.bfloat16)
    face_spec = face_spec.reshape(channels, FACES_OWN)
    spec_wide = face_spec.astype(jnp.float32)
    pressure = accumulate(
        obs_pos,
        lax.all_gather(spec_wide, "obs", axis=1, tiled=True),
        lax.all_gather(face_geom, "obs", axis=1, tiled=True),
    )
    rows_out = 2 * NFREQ // lax.axis_size("grp")
    summed = lax.psum(pressure, "grp")
    return lax.dynamic_slice_in_dim(summed, lax.axis_index("grp") * rows_out, rows_out, 0)


def solution(mesh):
    return jax.shard_map(
        local,
        mesh=mesh,
        in_specs=(
            P(None, None, ("grp", "obs")),
            P(("grp", "obs")),
            P(("grp", "obs")),
            P(None, ("grp", "obs")),
            P(None, "obs"),
        ),
        out_specs=P("grp", "obs"),
        check_vma=False,
    )
```

profile of v0, /device:TPU:0, one launch (start us, length us, event | category | flops | bytes accessed | tf_op | source)
XLA Modules:
  0.0 536.7 jit_solution(8264392097134709399)
XLA Ops:
  6.5 0.7 and_select_fusion
  8.0 0.7 copy.22
  8.7 8.0 %all-to-all-start.1 = ((s32[16,1,1]{2,1,0:T(1,128)}), s32[16,1,1]{2,1,0:T(1,128)S(1)}, u32[]{:S(2)}, u32[]{:S(2)}) async-start(s32[16,1,1]{2,1,0:T(1,128)} %copy.22), calls=%async_computation.1 | async-start | bytes 16384 | tf_op jit(solution)/shard_map/all_to_all | solution.py:99
  16.7 2.2 copy.28
  19.0 1.4 convolution_convert_fusion
  20.3 3.0 copy.21
  23.3 1.0 all-to-all-done.1
  24.3 6.3 %all-to-all-start = ((bf16[16,4,256,128]{3,2,1,0:T(8,128)(2,1)}), bf16[16,4,256,128]{3,2,1,0:T(8,128)(2,1)}, u32[]{:S(2)}, u32[]{:S(2)}) async-start(bf16[16,4,256,128]{3,2,1,0:T(8,128)(2,1)} %copy.21), calls=%async_computation | async-start | bytes 8388608 | tf_op jit(solution)/shard_map/all_to_all | solution.py:98
  30.9 0.4 reduce
  31.2 52.9 %all-to-all-done = bf16[16,4,256,128]{3,2,1,0:T(8,128)(2,1)} async-done(((bf16[16,4,256,128]{3,2,1,0:T(8,128)(2,1)}), bf16[16,4,256,128]{3,2,1,0:T(8,128)(2,1)}, u32[]{:S(2)}, u32[]{:S(2)}) %all-to-all-start) | async-done | bytes 4194336 | tf_op jit(solution)/shard_map/all_to_all | solution.py:98
  84.2 2.9 convolution_convert_fusion.1
  87.3 0.7 copy.34
  88.0 28.8 %all_gather.6 = f32[4,8192]{1,0:T(4,128)S(1)} all-gather(f32[4,512]{1,0:T(4,128)S(1)} %copy-done.1), channel_id=1, replica_groups=mesh['grp'=8,'obs'=16] {'obs'}, dimensions={1}, use_global_device_ids=true | all-gather | bytes 139264 | tf_op jit(solution)/shard_map/all_gather | solution.py:119
  116.8 27.1 %all-gather.2.cloned.1.call-done = f32[64,8192]{1,0:T(8,128)} async-done(((f32[64,512]{1,0:T(8,128)}), f32[64,8192]{1,0:T(8,128)}) %all-gather.2.cloned.1.call-update) | async-done | bytes 2097168 | tf_op jit(solution)/shard_map/all_gather | solution.py:118
  143.9 4.1 copy.30
  148.0 348.0 %while.11 = (s32[]{:T(128)}, f32[16,256]{1,0:T(8,128)S(1)}, f32[16,4,512]{2,1,0:T(4,128)S(1)}, f32[3,256]{1,0:T(4,128)S(1)}, f32[16,64,512]{2,0,1:T(8,128)}, /*index=5*/s32[]{:T(128)}, s32[]{:T(128)}, s32[]{}) while((s32[]{:T(128)}, f32[16,256]{1,0:T(8,128)S(1)}, f32[16,4,512]{2,1,0:T(4,128)S(1)}, f32[3,256]{1,0:T(4,128)S(1)}, ...), condition=%wide.region_6.7_spmd.clone, body=%wide.region_2.6_spmd.clone.sunk | while | flops 31997980 | bytes 12545307 | solution.py:75
  148.3 0.3 fusion.37
  148.6 1.3 constant_dynamic-slice_fusion.5
  150.2 19.5 %fusion.38 = (f32[8,256]{1,0:T(8,128)S(1)}, f32[8,256]{1,0:T(8,128)S(1)}) fusion(f32[8,512]{1,0:T(8,128)S(1)} %get-tuple-element.167, f32[256,512]{1,0:T(8,128)S(1)} %get-tuple-element.169, f32[8,512]{1,0:T(8,128)S(1)} %get-tuple-element.170, f32[8,512]{1,0:T(8,128)S(1)} %get-tuple-element.171, f32[8,512]{1,0:T(8,128)S(1)} %get-tuple-element.172, ...), kind=kLoop, calls=%fused_computation.8.clone.1 | loop fusion | flops 30404608 | bytes 3817504 | tf_op jit(solution)/shard_map/while/body/eval_jaxpr/reduce_sum | solution.py:55
  170.0 0.3 fusion.37
  170.4 1.3 constant_dynamic-slice_fusion.5
  172.0 19.5 %fusion.38 = (f32[8,256]{1,0:T(8,128)S(1)}, f32[8,256]{1,0:T(8,128)S(1)}) fusion(f32[8,512]{1,0:T(8,128)S(1)} %get-tuple-element.167, f32[256,512]{1,0:T(8,128)S(1)} %get-tuple-element.169, f32[8,512]{1,0:T(8,128)S(1)} %get-tuple-element.170, f32[8,512]{1,0:T(8,128)S(1)} %get-tuple-element.171, f32[8,512]{1,0:T(8,128)S(1)} %get-tuple-element.172, ...), kind=kLoop, calls=%fused_computation.8.clone.1 | loop fusion | flops 30404608 | bytes 3817504 | tf_op jit(solution)/shard_map/while/body/eval_jaxpr/reduce_sum | solution.py:55
  191.8 0.3 fusion.37
  192.1 1.3 constant_dynamic-slice_fusion.5
  193.7 19.5 %fusion.38 = (f32[8,256]{1,0:T(8,128)S(1)}, f32[8,256]{1,0:T(8,128)S(1)}) fusion(f32[8,512]{1,0:T(8,128)S(1)} %get-tuple-element.167, f32[256,512]{1,0:T(8,128)S(1)} %get-tuple-element.169, f32[8,512]{1,0:T(8,128)S(1)} %get-tuple-element.170, f32[8,512]{1,0:T(8,128)S(1)} %get-tuple-element.171, f32[8,512]{1,0:T(8,128)S(1)} %get-tuple-element.172, ...), kind=kLoop, calls=%fused_computation.8.clone.1 | loop fusion | flops 30404608 | bytes 3817504 | tf_op jit(solution)/shard_map/while/body/eval_jaxpr/reduce_sum | solution.py:55
  213.5 0.3 fusion.37
  213.9 1.3 constant_dynamic-slice_fusion.5
  215.5 19.5 %fusion.38 = (f32[8,256]{1,0:T(8,128)S(1)}, f32[8,256]{1,0:T(8,128)S(1)}) fusion(f32[8,512]{1,0:T(8,128)S(1)} %get-tuple-element.167, f32[256,512]{1,0:T(8,128)S(1)} %get-tuple-element.169, f32[8,512]{1,0:T(8,128)S(1)} %get-tuple-element.170, f32[8,512]{1,0:T(8,128)S(1)} %get-tuple-element.171, f32[8,512]{1,0:T(8,128)S(1)} %get-tuple-element.172, ...), kind=kLoop, calls=%fused_computation.8.clone.1 | loop fusion | flops 30404608 | bytes 3817504 | tf_op jit(solution)/shard_map/while/body/eval_jaxpr/reduce_sum | solution.py:55
  235.3 0.3 fusion.37
  235.6 1.3 constant_dynamic-slice_fusion.5
  237.2 19.5 %fusion.38 = (f32[8,256]{1,0:T(8,128)S(1)}, f32[8,256]{1,0:T(8,128)S(1)}) fusion(f32[8,512]{1,0:T(8,128)S(1)} %get-tuple-element.167, f32[256,512]{1,0:T(8,128)S(1)} %get-tuple-element.169, f32[8,512]{1,0:T(8,128)S(1)} %get-tuple-element.170, f32[8,512]{1,0:T(8,128)S(1)} %get-tuple-element.171, f32[8,512]{1,0:T(8,128)S(1)} %get-tuple-element.172, ...), kind=kLoop, calls=%fused_computation.8.clone.1 | loop fusion | flops 30404608 | bytes 3817504 | tf_op jit(solution)/shard_map/while/body/eval_jaxpr/reduce_sum | solution.py:55
  257.0 0.3 fusion.37
  257.4 1.3 constant_dynamic-slice_fusion.5
  259.0 19.5 %fusion.38 = (f32[8,256]{1,0:T(8,128)S(1)}, f32[8,256]{1,0:T(8,128)S(1)}) fusion(f32[8,512]{1,0:T(8,128)S(1)} %get-tuple-element.167, f32[256,512]{1,0:T(8,128)S(1)} %get-tuple-element.169, f32[8,512]{1,0:T(8,128)S(1)} %get-tuple-element.170, f32[8,512]{1,0:T(8,128)S(1)} %get-tuple-element.171, f32[8,512]{1,0:T(8,128)S(1)} %get-tuple-element.172, ...), kind=kLoop, calls=%fused_computation.8.clone.1 | loop fusion | flops 30404608 | bytes 3817504 | tf_op jit(solution)/shard_map/while/body/eval_jaxpr/reduce_sum | solution.py:55
  278.8 0.3 fusion.37
  279.1 1.3 constant_dynamic-slice_fusion.5
  280.7 19.5 %fusion.38 = (f32[8,256]{1,0:T(8,128)S(1)}, f32[8,256]{1,0:T(8,128)S(1)}) fusion(f32[8,512]{1,0:T(8,128)S(1)} %get-tuple-element.167, f32[256,512]{1,0:T(8,128)S(1)} %get-tuple-element.169, f32[8,512]{1,0:T(8,128)S(1)} %get-tuple-element.170, f32[8,512]{1,0:T(8,128)S(1)} %get-tuple-element.171, f32[8,512]{1,0:T(8,128)S(1)} %get-tuple-element.172, ...), kind=kLoop, calls=%fused_computation.8.clone.1 | loop fusion | flops 30404608 | bytes 3817504 | tf_op jit(solution)/shard_map/while/body/eval_jaxpr/reduce_sum | solution.py:55
  300.5 0.3 fusion.37
  300.9 1.3 constant_dynamic-slice_fusion.5
  302.5 19.5 %fusion.38 = (f32[8,256]{1,0:T(8,128)S(1)}, f32[8,256]{1,0:T(8,128)S(1)}) fusion(f32[8,512]{1,0:T(8,128)S(1)} %get-tuple-element.167, f32[256,512]{1,0:T(8,128)S(1)} %get-tuple-element.169, f32[8,512]{1,0:T(8,128)S(1)} %get-tuple-element.170, f32[8,512]{1,0:T(8,128)S(1)} %get-tuple-element.171, f32[8,512]{1,0:T(8,128)S(1)} %get-tuple-element.172, ...), kind=kLoop, calls=%fused_computation.8.clone.1 | loop fusion | flops 30404608 | bytes 3817504 | tf_op jit(solution)/shard_map/while/body/eval_jaxpr/reduce_sum | solution.py:55
  322.3 0.3 fusion.37
  322.6 1.3 constant_dynamic-slice_fusion.5
  324.2 19.5 %fusion.38 = (f32[8,256]{1,0:T(8,128)S(1)}, f32[8,256]{1,0:T(8,128)S(1)}) fusion(f32[8,512]{1,0:T(8,128)S(1)} %get-tuple-element.167, f32[256,512]{1,0:T(8,128)S(1)} %get-tuple-element.169, f32[8,512]{1,0:T(8,128)S(1)} %get-tuple-element.170, f32[8,512]{1,0:T(8,128)S(1)} %get-tuple-element.171, f32[8,512]{1,0:T(8,128)S(1)} %get-tuple-element.172, ...), kind=kLoop, calls=%fused_computation.8.clone.1 | loop fusion | flops 30404608 | bytes 3817504 | tf_op jit(solution)/shard_map/while/body/eval_jaxpr/reduce_sum | solution.py:55
  344.0 0.3 fusion.37
  344.4 1.3 constant_dynamic-slice_fusion.5
  346.0 19.5 %fusion.38 = (f32[8,256]{1,0:T(8,128)S(1)}, f32[8,256]{1,0:T(8,128)S(1)}) fusion(f32[8,512]{1,0:T(8,128)S(1)} %get-tuple-element.167, f32[256,512]{1,0:T(8,128)S(1)} %get-tuple-element.169, f32[8,512]{1,0:T(8,128)S(1)} %get-tuple-element.170, f32[8,512]{1,0:T(8,128)S(1)} %get-tuple-element.171, f32[8,512]{1,0:T(8,128)S(1)} %get-tuple-element.172, ...), kind=kLoop, calls=%fused_computation.8.clone.1 | loop fusion | flops 30404608 | bytes 3817504 | tf_op jit(solution)/shard_map/while/body/eval_jaxpr/reduce_sum | solution.py:55
  365.8 0.3 fusion.37
  366.1 1.3 constant_dynamic-slice_fusion.5
  367.7 19.5 %fusion.38 = (f32[8,256]{1,0:T(8,128)S(1)}, f32[8,256]{1,0:T(8,128)S(1)}) fusion(f32[8,512]{1,0:T(8,128)S(1)} %get-tuple-element.167, f32[256,512]{1,0:T(8,128)S(1)} %get-tuple-element.169, f32[8,512]{1,0:T(8,128)S(1)} %get-tuple-element.170, f32[8,512]{1,0:T(8,128)S(1)} %get-tuple-element.171, f32[8,512]{1,0:T(8,128)S(1)} %get-tuple-element.172, ...), kind=kLoop, calls=%fused_computation.8.clone.1 | loop fusion | flops 30404608 | bytes 3817504 | tf_op jit(solution)/shard_map/while/body/eval_jaxpr/reduce_sum | solution.py:55
  387.5 0.3 fusion.37
  387.9 1.3 constant_dynamic-slice_fusion.5
  389.5 19.5 %fusion.38 = (f32[8,256]{1,0:T(8,128)S(1)}, f32[8,256]{1,0:T(8,128)S(1)}) fusion(f32[8,512]{1,0:T(8,128)S(1)} %get-tuple-element.167, f32[256,512]{1,0:T(8,128)S(1)} %get-tuple-element.169, f32[8,512]{1,0:T(8,128)S(1)} %get-tuple-element.170, f32[8,512]{1,0:T(8,128)S(1)} %get-tuple-element.171, f32[8,512]{1,0:T(8,128)S(1)} %get-tuple-element.172, ...), kind=kLoop, calls=%fused_computation.8.clone.1 | loop fusion | flops 30404608 | bytes 3817504 | tf_op jit(solution)/shard_map/while/body/eval_jaxpr/reduce_sum | solution.py:55
  409.6 1.3 constant_dynamic-slice_fusion.5
  411.2 19.5 %fusion.38 = (f32[8,256]{1,0:T(8,128)S(1)}, f32[8,256]{1,0:T(8,128)S(1)}) fusion(f32[8,512]{1,0:T(8,128)S(1)} %get-tuple-element.167, f32[256,512]{1,0:T(8,128)S(1)} %get-tuple-element.169, f32[8,512]{1,0:T(8,128)S(1)} %get-tuple-element.170, f32[8,512]{1,0:T(8,128)S(1)} %get-tuple-element.171, f32[8,512]{1,0:T(8,128)S(1)} %get-tuple-element.172, ...), kind=kLoop, calls=%fused_computation.8.clone.1 | loop fusion | flops 30404608 | bytes 3817504 | tf_op jit(solution)/shard_map/while/body/eval_jaxpr/reduce_sum | solution.py:55
  431.0 0.3 fusion.37
  431.3 1.3 constant_dynamic-slice_fusion.5
  432.9 19.5 %fusion.38 = (f32[8,256]{1,0:T(8,128)S(1)}, f32[8,256]{1,0:T(8,128)S(1)}) fusion(f32[8,512]{1,0:T(8,128)S(1)} %get-tuple-element.167, f32[256,512]{1,0:T(8,128)S(1)} %get-tuple-element.169, f32[8,512]{1,0:T(8,128)S(1)} %get-tuple-element.170, f32[8,512]{1,0:T(8,128)S(1)} %get-tuple-element.171, f32[8,512]{1,0:T(8,128)S(1)} %get-tuple-element.172, ...), kind=kLoop, calls=%fused_computation.8.clone.1 | loop fusion | flops 30404608 | bytes 3817504 | tf_op jit(solution)/shard_map/while/body/eval_jaxpr/reduce_sum | solution.py:55
  452.8 0.3 fusion.37
  453.1 1.3 constant_dynamic-slice_fusion.5
  454.7 19.5 %fusion.38 = (f32[8,256]{1,0:T(8,128)S(1)}, f32[8,256]{1,0:T(8,128)S(1)}) fusion(f32[8,512]{1,0:T(8,128)S(1)} %get-tuple-element.167, f32[256,512]{1,0:T(8,128)S(1)} %get-tuple-element.169, f32[8,512]{1,0:T(8,128)S(1)} %get-tuple-element.170, f32[8,512]{1,0:T(8,128)S(1)} %get-tuple-element.171, f32[8,512]{1,0:T(8,128)S(1)} %get-tuple-element.172, ...), kind=kLoop, calls=%fused_computation.8.clone.1 | loop fusion | flops 30404608 | bytes 3817504 | tf_op jit(solution)/shard_map/while/body/eval_jaxpr/reduce_sum | solution.py:55
  474.8 1.3 constant_dynamic-slice_fusion.5
  476.4 19.5 %fusion.38 = (f32[8,256]{1,0:T(8,128)S(1)}, f32[8,256]{1,0:T(8,128)S(1)}) fusion(f32[8,512]{1,0:T(8,128)S(1)} %get-tuple-element.167, f32[256,512]{1,0:T(8,128)S(1)} %get-tuple-element.169, f32[8,512]{1,0:T(8,128)S(1)} %get-tuple-element.170, f32[8,512]{1,0:T(8,128)S(1)} %get-tuple-element.171, f32[8,512]{1,0:T(8,128)S(1)} %get-tuple-element.172, ...), kind=kLoop, calls=%fused_computation.8.clone.1 | loop fusion | flops 30404608 | bytes 3817504 | tf_op jit(solution)/shard_map/while/body/eval_jaxpr/reduce_sum | solution.py:55
  496.0 33.3 %psum.7 = f32[16,256]{1,0:T(8,128)S(1)} all-reduce(f32[16,256]{1,0:T(8,128)S(1)} %get-tuple-element.32), channel_id=1, replica_groups=mesh['grp'=8,'obs'=16] {'grp'}, use_global_device_ids=true, to_apply=%region_7.8 | all-reduce | flops 4096 | bytes 32768 | tf_op jit(solution)/shard_map/psum | solution.py:122
  529.3 0.6 constant_dynamic-slice_fusion.2
  (161 shorter events, 9.1 us)
Async XLA Ops:
  8.7 15.6 %all-to-all-start.1 = ((s32[16,1,1]{2,1,0:T(1,128)}), s32[16,1,1]{2,1,0:T(1,128)S(1)}, u32[]{:S(2)}, u32[]{:S(2)}) async-start(s32[16,1,1]{2,1,0:T(1,128)} %copy.22), calls=%async_computation.1 | async-start | bytes 16384 | tf_op jit(solution)/shard_map/all_to_all | solution.py:99
  24.3 59.8 %all-to-all-start = ((bf16[16,4,256,128]{3,2,1,0:T(8,128)(2,1)}), bf16[16,4,256,128]{3,2,1,0:T(8,128)(2,1)}, u32[]{:S(2)}, u32[]{:S(2)}) async-start(bf16[16,4,256,128]{3,2,1,0:T(8,128)(2,1)} %copy.21), calls=%async_computation | async-start | bytes 8388608 | tf_op jit(solution)/shard_map/all_to_all | solution.py:98
  30.6 57.4 %copy-start.1 = (f32[4,512]{1,0:T(4,128)S(1)}, f32[4,512]{1,0:T(4,128)}, u32[]{:S(2)}) copy-start(f32[4,512]{1,0:T(4,128)} %param.10) | copy-start | bytes 24580
  30.6 113.3 %all-gather.2.cloned.1.call-start = ((), (), s32[]{:S(2)}) async-start(), calls=%async_computation.2 | async-start | bytes 2228224 | tf_op jit(solution)/shard_map/all_gather | solution.py:118
  84.2 63.9 %copy-start = (f32[3,256]{1,0:T(4,128)S(1)}, f32[3,256]{1,0:T(4,128)}, u32[]{:S(2)}) copy-start(f32[3,256]{1,0:T(4,128)} %param.11) | copy-start | bytes 9220
Sparse Core Ops, SparseCore 0:
  88.1 55.7 all-gather.1
where the time goes:
time: 538 us; the launch traced here: 537 us
  other arithmetic  324 us (60%)
  waiting for transfers between devices  81 us (15%)
  blocking collectives  62 us (12%)
  local copies, waits for them, and re-layouts  35.4 us (7%)
  starting transfers between devices  14.3 us (3%)
  between operations  14.1 us (3%)
    reduce_sum x16, other arithmetic, pressure_tiles(): press_re = jnp.sum(green_re * bracket_re - green_im * bracket_im, axis=2)  312 us
    all_to_all x1, waiting for transfers between devices, local(): lax.all_to_all(outgoing, 'obs', split_axis=0, concat_axis=0, tiled=True)  52.9 us
    psum x1, blocking collectives, local(): summed = lax.psum(pressure, 'grp')  33.3 us
    all_gather x1, blocking collectives, local(): lax.all_gather(face_geom, 'obs', axis=1, tiled=True)  28.8 us
    all_gather x1, waiting for transfers between devices, local(): lax.all_gather(spec_wide, 'obs', axis=1, tiled=True)  27.1 us
    dynamic_slice x32, local copies, waits for them, and re-layouts, accumulate(): result, _ = lax.scan(add_block, zero_sum, (spec_blocks, geom_blocks))  21.7 us
  transfers between devices with their start and end apart: 3, of which 3 were waited for; matrix products, arithmetic and copies ran while one was open for 1% of the time, Pallas kernels for 0%

commit v1 on v0

--- a/solution.py
+++ b/solution.py
@@ -3,6 +3,7 @@
 import jax.numpy as jnp
 from jax import lax
 from jax.sharding import PartitionSpec as P
+from jax.lax import all_to_all, psum
 
 SAMPLES = 256
 NFREQ = 8
@@ -113,10 +114,17 @@
     ).astype(jnp.bfloat16)
     face_spec = face_spec.reshape(channels, FACES_OWN)
     spec_wide = face_spec.astype(jnp.float32)
+    plan_core_on = lambda m, dim_i: jnp.concatenate(
+        all_to_all(
+            jnp.stack([m for _ in range(psum(1, axis_name="obs"))], 0),
+            axis_name="obs",
+            split_axis=0,
+            concat_axis=0,
+        ),
+        dim_i,
+    )
     pressure = accumulate(
-        obs_pos,
-        lax.all_gather(spec_wide, "obs", axis=1, tiled=True),
-        lax.all_gather(face_geom, "obs", axis=1, tiled=True),
+        obs_pos, plan_core_on(spec_wide, 1), lax.all_gather(face_geom, "obs", axis=1, tiled=True)
     )
     rows_out = 2 * NFREQ // lax.axis_size("grp")
     summed = lax.psum(pressure, "grp")

time: 538 us -> 514 us (0.955)
  waiting for transfers between devices: 81 us -> 54 us
  blocking collectives: 62 us -> 76.4 us
  between operations: 14.1 us -> 0.76 us
  starting transfers between devices: 14.3 us -> 27.2 us
  local copies, waits for them, and re-layouts: 35.4 us -> 25.2 us
    all_gather x1 -> x0, waiting for transfers between devices: 27.1 us -> none  [local(): lax.all_gather(spec_wide, 'obs', axis=1, tiled=True)]
    all_gather x1, blocking collectives: 28.8 us -> 42.7 us  [local(): lax.all_gather(face_geom, 'obs', axis=1, tiled=True)]
    all_to_all x0 -> x1, starting transfers between devices: none -> 12.9 us  [local(): all_to_all(jnp.stack([m for _ in range(psum(1, axis_name='obs'))], 0), ax...]
    dynamic_slice x32 -> x16, local copies, waits for them, and re-layouts: 21.7 us -> 14.7 us  [accumulate(): result, _ = lax.scan(add_block, zero_sum, (spec_blocks, geom_blocks))]
  transfers between devices with their start and end apart: 3 -> 3, of which waited for: 3 -> 2; matrix products, arithmetic and copies ran while one was open for 1% -> 1% of each run, Pallas kernels for 0% -> 0%
where the time goes in v1:
time: 514 us; the launch traced here: 513 us
  other arithmetic  324 us (63%)
  blocking collectives  76.4 us (15%)
  waiting for transfers between devices  54 us (11%)
  starting transfers between devices  27.2 us (5%)
  local copies, waits for them, and re-layouts  25.2 us (5%)
    reduce_sum x16, other arithmetic, pressure_tiles(): press_re = jnp.sum(green_re * bracket_re - green_im * bracket_im, axis=2)  312 us
    all_to_all x1, waiting for transfers between devices, local(): lax.all_to_all(outgoing, 'obs', split_axis=0, concat_axis=0, tiled=True)  53 us
    all_gather x1, blocking collectives, local(): lax.all_gather(face_geom, 'obs', axis=1, tiled=True)  42.7 us
    psum x1, blocking collectives, local(): summed = lax.psum(pressure, 'grp')  33.7 us
    dynamic_slice x16, local copies, waits for them, and re-layouts, accumulate(): result, _ = lax.scan(add_block, zero_sum, (spec_blocks, geom_blocks))  14.7 us
    all_to_all x1, starting transfers between devices, local(): all_to_all(jnp.stack([m for _ in range(psum(1, axis_name='obs'))], 0), ax...  12.9 us
  transfers between devices with their start and end apart: 3, of which 2 were waited for; matrix products, arithmetic and copies ran while one was open for 1% of the time, Pallas kernels for 0%

profile of v1, /device:TPU:0, one launch (start us, length us, event | category | flops | bytes accessed | tf_op | source)
XLA Modules:
  0.0 513.0 jit_solution(12713163079595226304)
XLA Ops:
  0.0 0.7 and_select_fusion
  1.5 0.7 copy.16
  2.2 8.0 %all-to-all-start.1 = ((s32[16,1,1]{2,1,0:T(1,128)}), s32[16,1,1]{2,1,0:T(1,128)S(1)}, u32[]{:S(2)}, u32[]{:S(2)}) async-start(s32[16,1,1]{2,1,0:T(1,128)} %copy.16), calls=%async_computation.1 | async-start | bytes 16384 | tf_op jit(solution)/shard_map/all_to_all | solution.py:100
  10.2 2.2 copy.20
  12.4 1.4 convolution_convert_fusion
  13.8 3.0 copy.15
  16.8 1.0 all-to-all-done.1
  17.8 6.3 %all-to-all-start = ((bf16[16,4,256,128]{3,2,1,0:T(8,128)(2,1)}), bf16[16,4,256,128]{3,2,1,0:T(8,128)(2,1)}, u32[]{:S(2)}, u32[]{:S(2)}) async-start(bf16[16,4,256,128]{3,2,1,0:T(8,128)(2,1)} %copy.15), calls=%async_computation | async-start | bytes 8388608 | tf_op jit(solution)/shard_map/all_to_all | solution.py:99
  24.3 0.4 reduce
  24.6 53.0 %all-to-all-done = bf16[16,4,256,128]{3,2,1,0:T(8,128)(2,1)} async-done(((bf16[16,4,256,128]{3,2,1,0:T(8,128)(2,1)}), bf16[16,4,256,128]{3,2,1,0:T(8,128)(2,1)}, u32[]{:S(2)}, u32[]{:S(2)}) %all-to-all-start) | async-done | bytes 4194336 | tf_op jit(solution)/shard_map/all_to_all | solution.py:99
  77.6 2.8 convolution_convert_fusion.1
  80.8 1.6 stack.2
  82.3 12.9 %all-to-all-start.2 = ((f32[16,64,512]{2,1,0:T(8,128)}), f32[16,64,512]{2,1,0:T(8,128)}, u32[]{:S(2)}, u32[]{:S(2)}) async-start(f32[16,64,512]{2,1,0:T(8,128)} %stack.2), calls=%async_computation.2 | async-start | bytes 4194304 | tf_op jit(solution)/shard_map/all_to_all | solution.py:118
  95.2 42.7 %all_gather.3 = f32[4,8192]{1,0:T(4,128)S(1)} all-gather(f32[4,512]{1,0:T(4,128)S(1)} %copy-done.1), channel_id=1, replica_groups=mesh['grp'=8,'obs'=16] {'obs'}, dimensions={1}, use_global_device_ids=true | all-gather | bytes 139264 | tf_op jit(solution)/shard_map/all_gather | solution.py:127
  137.9 340.9 %while.11 = (s32[]{:T(128)}, f32[16,256]{1,0:T(8,128)S(1)}, f32[16,4,512]{2,1,0:T(4,128)S(1)}, f32[3,256]{1,0:T(4,128)S(1)}, f32[16,64,512]{2,1,0:T(8,128)}, /*index=5*/s32[]{:T(128)}, s32[]{:T(128)}, s32[]{}) while((s32[]{:T(128)}, f32[16,256]{1,0:T(8,128)S(1)}, f32[16,4,512]{2,1,0:T(4,128)S(1)}, f32[3,256]{1,0:T(4,128)S(1)}, ...), condition=%wide.region_6.7_spmd.clone, body=%wide.region_2.6_spmd.clone.sunk | while | flops 31997980 | bytes 12283163 | solution.py:76
  138.1 0.3 fusion.37
  138.4 0.9 constant_dynamic-slice_fusion.5
  139.6 19.5 %fusion.38 = (f32[8,256]{1,0:T(8,128)S(1)}, f32[8,256]{1,0:T(8,128)S(1)}) fusion(f32[8,512]{1,0:T(8,128)S(1)} %get-tuple-element.142, f32[256,512]{1,0:T(8,128)S(1)} %get-tuple-element.144, f32[8,512]{1,0:T(8,128)S(1)} %get-tuple-element.145, f32[8,512]{1,0:T(8,128)S(1)} %get-tuple-element.146, f32[8,512]{1,0:T(8,128)S(1)} %get-tuple-element.147, ...), kind=kLoop, calls=%fused_computation.8.clone.1 | loop fusion | flops 30404608 | bytes 3817504 | tf_op jit(solution)/shard_map/while/body/eval_jaxpr/reduce_sum | solution.py:56
  159.4 0.3 fusion.37
  159.8 0.9 constant_dynamic-slice_fusion.5
  160.9 19.5 %fusion.38 = (f32[8,256]{1,0:T(8,128)S(1)}, f32[8,256]{1,0:T(8,128)S(1)}) fusion(f32[8,512]{1,0:T(8,128)S(1)} %get-tuple-element.142, f32[256,512]{1,0:T(8,128)S(1)} %get-tuple-element.144, f32[8,512]{1,0:T(8,128)S(1)} %get-tuple-element.145, f32[8,512]{1,0:T(8,128)S(1)} %get-tuple-element.146, f32[8,512]{1,0:T(8,128)S(1)} %get-tuple-element.147, ...), kind=kLoop, calls=%fused_computation.8.clone.1 | loop fusion | flops 30404608 | bytes 3817504 | tf_op jit(solution)/shard_map/while/body/eval_jaxpr/reduce_sum | solution.py:56
  180.7 0.3 fusion.37
  181.1 0.9 constant_dynamic-slice_fusion.5
  182.2 19.5 %fusion.38 = (f32[8,256]{1,0:T(8,128)S(1)}, f32[8,256]{1,0:T(8,128)S(1)}) fusion(f32[8,512]{1,0:T(8,128)S(1)} %get-tuple-element.142, f32[256,512]{1,0:T(8,128)S(1)} %get-tuple-element.144, f32[8,512]{1,0:T(8,128)S(1)} %get-tuple-element.145, f32[8,512]{1,0:T(8,128)S(1)} %get-tuple-element.146, f32[8,512]{1,0:T(8,128)S(1)} %get-tuple-element.147, ...), kind=kLoop, calls=%fused_computation.8.clone.1 | loop fusion | flops 30404608 | bytes 3817504 | tf_op jit(solution)/shard_map/while/body/eval_jaxpr/reduce_sum | solution.py:56
  202.1 0.3 fusion.37
  202.4 0.9 constant_dynamic-slice_fusion.5
  203.5 19.5 %fusion.38 = (f32[8,256]{1,0:T(8,128)S(1)}, f32[8,256]{1,0:T(8,128)S(1)}) fusion(f32[8,512]{1,0:T(8,128)S(1)} %get-tuple-element.142, f32[256,512]{1,0:T(8,128)S(1)} %get-tuple-element.144, f32[8,512]{1,0:T(8,128)S(1)} %get-tuple-element.145, f32[8,512]{1,0:T(8,128)S(1)} %get-tuple-element.146, f32[8,512]{1,0:T(8,128)S(1)} %get-tuple-element.147, ...), kind=kLoop, calls=%fused_computation.8.clone.1 | loop fusion | flops 30404608 | bytes 3817504 | tf_op jit(solution)/shard_map/while/body/eval_jaxpr/reduce_sum | solution.py:56
  223.4 0.3 fusion.37
  223.7 0.9 constant_dynamic-slice_fusion.5
  224.8 19.5 %fusion.38 = (f32[8,256]{1,0:T(8,128)S(1)}, f32[8,256]{1,0:T(8,128)S(1)}) fusion(f32[8,512]{1,0:T(8,128)S(1)} %get-tuple-element.142, f32[256,512]{1,0:T(8,128)S(1)} %get-tuple-element.144, f32[8,512]{1,0:T(8,128)S(1)} %get-tuple-element.145, f32[8,512]{1,0:T(8,128)S(1)} %get-tuple-element.146, f32[8,512]{1,0:T(8,128)S(1)} %get-tuple-element.147, ...), kind=kLoop, calls=%fused_computation.8.clone.1 | loop fusion | flops 30404608 | bytes 3817504 | tf_op jit(solution)/shard_map/while/body/eval_jaxpr/reduce_sum | solution.py:56
  244.7 0.3 fusion.37
  245.0 0.9 constant_dynamic-slice_fusion.5
  246.1 19.5 %fusion.38 = (f32[8,256]{1,0:T(8,128)S(1)}, f32[8,256]{1,0:T(8,128)S(1)}) fusion(f32[8,512]{1,0:T(8,128)S(1)} %get-tuple-element.142, f32[256,512]{1,0:T(8,128)S(1)} %get-tuple-element.144, f32[8,512]{1,0:T(8,128)S(1)} %get-tuple-element.145, f32[8,512]{1,0:T(8,128)S(1)} %get-tuple-element.146, f32[8,512]{1,0:T(8,128)S(1)} %get-tuple-element.147, ...), kind=kLoop, calls=%fused_computation.8.clone.1 | loop fusion | flops 30404608 | bytes 3817504 | tf_op jit(solution)/shard_map/while/body/eval_jaxpr/reduce_sum | solution.py:56
  266.0 0.3 fusion.37
  266.3 0.9 constant_dynamic-slice_fusion.5
  267.4 19.5 %fusion.38 = (f32[8,256]{1,0:T(8,128)S(1)}, f32[8,256]{1,0:T(8,128)S(1)}) fusion(f32[8,512]{1,0:T(8,128)S(1)} %get-tuple-element.142, f32[256,512]{1,0:T(8,128)S(1)} %get-tuple-element.144, f32[8,512]{1,0:T(8,128)S(1)} %get-tuple-element.145, f32[8,512]{1,0:T(8,128)S(1)} %get-tuple-element.146, f32[8,512]{1,0:T(8,128)S(1)} %get-tuple-element.147, ...), kind=kLoop, calls=%fused_computation.8.clone.1 | loop fusion | flops 30404608 | bytes 3817504 | tf_op jit(solution)/shard_map/while/body/eval_jaxpr/reduce_sum | solution.py:56
  287.3 0.3 fusion.37
  287.6 0.9 constant_dynamic-slice_fusion.5
  288.8 19.5 %fusion.38 = (f32[8,256]{1,0:T(8,128)S(1)}, f32[8,256]{1,0:T(8,128)S(1)}) fusion(f32[8,512]{1,0:T(8,128)S(1)} %get-tuple-element.142, f32[256,512]{1,0:T(8,128)S(1)} %get-tuple-element.144, f32[8,512]{1,0:T(8,128)S(1)} %get-tuple-element.145, f32[8,512]{1,0:T(8,128)S(1)} %get-tuple-element.146, f32[8,512]{1,0:T(8,128)S(1)} %get-tuple-element.147, ...), kind=kLoop, calls=%fused_computation.8.clone.1 | loop fusion | flops 30404608 | bytes 3817504 | tf_op jit(solution)/shard_map/while/body/eval_jaxpr/reduce_sum | solution.py:56
  308.6 0.3 fusion.37
  308.9 0.9 constant_dynamic-slice_fusion.5
  310.1 19.5 %fusion.38 = (f32[8,256]{1,0:T(8,128)S(1)}, f32[8,256]{1,0:T(8,128)S(1)}) fusion(f32[8,512]{1,0:T(8,128)S(1)} %get-tuple-element.142, f32[256,512]{1,0:T(8,128)S(1)} %get-tuple-element.144, f32[8,512]{1,0:T(8,128)S(1)} %get-tuple-element.145, f32[8,512]{1,0:T(8,128)S(1)} %get-tuple-element.146, f32[8,512]{1,0:T(8,128)S(1)} %get-tuple-element.147, ...), kind=kLoop, calls=%fused_computation.8.clone.1 | loop fusion | flops 30404608 | bytes 3817504 | tf_op jit(solution)/shard_map/while/body/eval_jaxpr/reduce_sum | solution.py:56
  329.9 0.3 fusion.37
  330.2 0.9 constant_dynamic-slice_fusion.5
  331.4 19.5 %fusion.38 = (f32[8,256]{1,0:T(8,128)S(1)}, f32[8,256]{1,0:T(8,128)S(1)}) fusion(f32[8,512]{1,0:T(8,128)S(1)} %get-tuple-element.142, f32[256,512]{1,0:T(8,128)S(1)} %get-tuple-element.144, f32[8,512]{1,0:T(8,128)S(1)} %get-tuple-element.145, f32[8,512]{1,0:T(8,128)S(1)} %get-tuple-element.146, f32[8,512]{1,0:T(8,128)S(1)} %get-tuple-element.147, ...), kind=kLoop, calls=%fused_computation.8.clone.1 | loop fusion | flops 30404608 | bytes 3817504 | tf_op jit(solution)/shard_map/while/body/eval_jaxpr/reduce_sum | solution.py:56
  351.2 0.3 fusion.37
  351.5 0.9 constant_dynamic-slice_fusion.5
  352.7 19.5 %fusion.38 = (f32[8,256]{1,0:T(8,128)S(1)}, f32[8,256]{1,0:T(8,128)S(1)}) fusion(f32[8,512]{1,0:T(8,128)S(1)} %get-tuple-element.142, f32[256,512]{1,0:T(8,128)S(1)} %get-tuple-element.144, f32[8,512]{1,0:T(8,128)S(1)} %get-tuple-element.145, f32[8,512]{1,0:T(8,128)S(1)} %get-tuple-element.146, f32[8,512]{1,0:T(8,128)S(1)} %get-tuple-element.147, ...), kind=kLoop, calls=%fused_computation.8.clone.1 | loop fusion | flops 30404608 | bytes 3817504 | tf_op jit(solution)/shard_map/while/body/eval_jaxpr/reduce_sum | solution.py:56
  372.8 0.9 constant_dynamic-slice_fusion.5
  374.0 19.5 %fusion.38 = (f32[8,256]{1,0:T(8,128)S(1)}, f32[8,256]{1,0:T(8,128)S(1)}) fusion(f32[8,512]{1,0:T(8,128)S(1)} %get-tuple-element.142, f32[256,512]{1,0:T(8,128)S(1)} %get-tuple-element.144, f32[8,512]{1,0:T(8,128)S(1)} %get-tuple-element.145, f32[8,512]{1,0:T(8,128)S(1)} %get-tuple-element.146, f32[8,512]{1,0:T(8,128)S(1)} %get-tuple-element.147, ...), kind=kLoop, calls=%fused_computation.8.clone.1 | loop fusion | flops 30404608 | bytes 3817504 | tf_op jit(solution)/shard_map/while/body/eval_jaxpr/reduce_sum | solution.py:56
  393.8 0.3 fusion.37
  394.1 0.9 constant_dynamic-slice_fusion.5
  395.3 19.5 %fusion.38 = (f32[8,256]{1,0:T(8,128)S(1)}, f32[8,256]{1,0:T(8,128)S(1)}) fusion(f32[8,512]{1,0:T(8,128)S(1)} %get-tuple-element.142, f32[256,512]{1,0:T(8,128)S(1)} %get-tuple-element.144, f32[8,512]{1,0:T(8,128)S(1)} %get-tuple-element.145, f32[8,512]{1,0:T(8,128)S(1)} %get-tuple-element.146, f32[8,512]{1,0:T(8,128)S(1)} %get-tuple-element.147, ...), kind=kLoop, calls=%fused_computation.8.clone.1 | loop fusion | flops 30404608 | bytes 3817504 | tf_op jit(solution)/shard_map/while/body/eval_jaxpr/reduce_sum | solution.py:56
  415.1 0.3 fusion.37
  415.4 0.9 constant_dynamic-slice_fusion.5
  416.6 19.5 %fusion.38 = (f32[8,256]{1,0:T(8,128)S(1)}, f32[8,256]{1,0:T(8,128)S(1)}) fusion(f32[8,512]{1,0:T(8,128)S(1)} %get-tuple-element.142, f32[256,512]{1,0:T(8,128)S(1)} %get-tuple-element.144, f32[8,512]{1,0:T(8,128)S(1)} %get-tuple-element.145, f32[8,512]{1,0:T(8,128)S(1)} %get-tuple-element.146, f32[8,512]{1,0:T(8,128)S(1)} %get-tuple-element.147, ...), kind=kLoop, calls=%fused_computation.8.clone.1 | loop fusion | flops 30404608 | bytes 3817504 | tf_op jit(solution)/shard_map/while/body/eval_jaxpr/reduce_sum | solution.py:56
  436.4 0.3 fusion.37
  436.7 0.9 constant_dynamic-slice_fusion.5
  437.9 19.5 %fusion.38 = (f32[8,256]{1,0:T(8,128)S(1)}, f32[8,256]{1,0:T(8,128)S(1)}) fusion(f32[8,512]{1,0:T(8,128)S(1)} %get-tuple-element.142, f32[256,512]{1,0:T(8,128)S(1)} %get-tuple-element.144, f32[8,512]{1,0:T(8,128)S(1)} %get-tuple-element.145, f32[8,512]{1,0:T(8,128)S(1)} %get-tuple-element.146, f32[8,512]{1,0:T(8,128)S(1)} %get-tuple-element.147, ...), kind=kLoop, calls=%fused_computation.8.clone.1 | loop fusion | flops 30404608 | bytes 3817504 | tf_op jit(solution)/shard_map/while/body/eval_jaxpr/reduce_sum | solution.py:56
  457.7 0.3 fusion.37
  458.0 0.9 constant_dynamic-slice_fusion.5
  459.2 19.5 %fusion.38 = (f32[8,256]{1,0:T(8,128)S(1)}, f32[8,256]{1,0:T(8,128)S(1)}) fusion(f32[8,512]{1,0:T(8,128)S(1)} %get-tuple-element.142, f32[256,512]{1,0:T(8,128)S(1)} %get-tuple-element.144, f32[8,512]{1,0:T(8,128)S(1)} %get-tuple-element.145, f32[8,512]{1,0:T(8,128)S(1)} %get-tuple-element.146, f32[8,512]{1,0:T(8,128)S(1)} %get-tuple-element.147, ...), kind=kLoop, calls=%fused_computation.8.clone.1 | loop fusion | flops 30404608 | bytes 3817504 | tf_op jit(solution)/shard_map/while/body/eval_jaxpr/reduce_sum | solution.py:56
  478.8 33.7 %psum.7 = f32[16,256]{1,0:T(8,128)S(1)} all-reduce(f32[16,256]{1,0:T(8,128)S(1)} %get-tuple-element.32), channel_id=1, replica_groups=mesh['grp'=8,'obs'=16] {'grp'}, use_global_device_ids=true, to_apply=%region_7.8 | all-reduce | flops 4096 | bytes 32768 | tf_op jit(solution)/shard_map/psum | solution.py:130
  512.5 0.6 constant_dynamic-slice_fusion.2
  (144 shorter events, 8.6 us)
Async XLA Ops:
  2.2 15.6 %all-to-all-start.1 = ((s32[16,1,1]{2,1,0:T(1,128)}), s32[16,1,1]{2,1,0:T(1,128)S(1)}, u32[]{:S(2)}, u32[]{:S(2)}) async-start(s32[16,1,1]{2,1,0:T(1,128)} %copy.16), calls=%async_computation.1 | async-start | bytes 16384 | tf_op jit(solution)/shard_map/all_to_all | solution.py:100
  17.8 59.8 %all-to-all-start = ((bf16[16,4,256,128]{3,2,1,0:T(8,128)(2,1)}), bf16[16,4,256,128]{3,2,1,0:T(8,128)(2,1)}, u32[]{:S(2)}, u32[]{:S(2)}) async-start(bf16[16,4,256,128]{3,2,1,0:T(8,128)(2,1)} %copy.15), calls=%async_computation | async-start | bytes 8388608 | tf_op jit(solution)/shard_map/all_to_all | solution.py:99
  80.5 14.7 %copy-start.1 = (f32[4,512]{1,0:T(4,128)S(1)}, f32[4,512]{1,0:T(4,128)}, u32[]{:S(2)}) copy-start(f32[4,512]{1,0:T(4,128)} %param.10) | copy-start | bytes 24580
  80.5 57.4 %copy-start = (f32[3,256]{1,0:T(4,128)S(1)}, f32[3,256]{1,0:T(4,128)}, u32[]{:S(2)}) copy-start(f32[3,256]{1,0:T(4,128)} %param.11) | copy-start | bytes 9220
  82.3 55.6 %all-to-all-start.2 = ((f32[16,64,512]{2,1,0:T(8,128)}), f32[16,64,512]{2,1,0:T(8,128)}, u32[]{:S(2)}, u32[]{:S(2)}) async-start(f32[16,64,512]{2,1,0:T(8,128)} %stack.2), calls=%async_computation.2 | async-start | bytes 4194304 | tf_op jit(solution)/shard_map/all_to_all | solution.py:118
